TPU v7x, 32 devices: a whole 2x2x4 slice. The times are simulated.
32 devices in a mesh: band: 8 (over z, x), dom: 4 (over y, core).
Axes of the slice: x: 2, y: 2, z: 4, core: 2. Of those that a mesh axis runs over, the one named last changes fastest.
Arguments:
- orbitals: bfloat16 [512, 16, 2048], P('band', 'dom'), may hold values from -6 to 6
- potential: float32 [16, 2048], P('dom'), may hold values from 0 to 2
- bounds: float32 [2], replicated, may hold values from 1 to 10, as said below
Outputs:
- rotated: bfloat16 [512, 16, 2048], P('band', 'dom')
- projected: float32 [512, 512], replicated
Inputs may be any that keep to these rules, and one draw needn't show every extreme that they name: bounds[0] lies in 1 to 2 and bounds[1] in 8.5 to 10, above the whole spectrum of H.
All inputs are finite; a program needn't handle non-finite values.
Results may differ from a plain program's by a relative error of at most 0.006.
Values may be sent and summed in bfloat16 or wider, within the bound.
A program may use at most 128 MiB of HBM per device.

v0:
```python
import jax
import jax.numpy as jnp
from jax import lax
from jax.sharding import PartitionSpec as P

BANDS = 512
GRID_Y = 64
GRID_Z = 32
DEG = 8
NS_STEPS = 8


def padded(cells, sides, width):
    for axis, dim in sides:
        count = lax.axis_size(axis)
        head = lax.slice_in_dim(cells, 0, width, axis=dim)
        tail = lax.slice_in_dim(cells, cells.shape[dim] - width, cells.shape[dim], axis=dim)
        cells = jnp.concatenate(
            [
                lax.ppermute(tail, axis, [(i, (i + 1) % count) for i in range(count)]),
                cells,
                lax.ppermute(head, axis, [((i + 1) % count, i) for i in range(count)]),
            ],
            axis=dim,
        )
    return cells


def planes(field):
    return field.reshape(field.shape[0], field.shape[1], GRID_Y, GRID_Z)


def flatten(field):
    return field.reshape(field.shape[0], field.shape[1], GRID_Y * GRID_Z)


def stencil(widened, pot_planes):
    middle = widened[:, 1:-1]
    beside = widened[:, 2:] + widened[:, :-2]
    beside = beside + jnp.roll(middle, -1, 2) + jnp.roll(middle, 1, 2)
    beside = beside + jnp.roll(middle, -1, 3) + jnp.roll(middle, 1, 3)
    return -0.5 * (beside - 6.0 * middle) + pot_planes * middle


def slab_filter(start, potential, half_width, centre):
    slab = start.shape[1]
    pot_inner = potential.reshape(slab, GRID_Y, GRID_Z)

    def apply_once(field):
        widened = padded(field, (("dom", 1),), 1)
        return flatten(stencil(planes(widened), pot_inner))

    earlier = start
    current = (apply_once(start) - centre * start) / half_width
    for repeat in range(DEG - 1):
        following = 2.0 * (apply_once(current) - centre * current) / half_width - earlier
        earlier = current
        current = following
    applied = apply_once(current)
    return (current, applied)


def gram_pair(point_filt, point_applied, cell_volume):
    contract = (((1,), (1,)), ((), ()))
    correlation_part = (
        lax.dot_general(point_filt, point_filt, contract, preferred_element_type=jnp.float32)
        * cell_volume
    )
    hamil_part = (
        lax.dot_general(point_filt, point_applied, contract, preferred_element_type=jnp.float32)
        * cell_volume
    )
    return lax.psum((correlation_part, hamil_part), ("band", "dom"))


def body(orbitals, potential, bounds):
    local_bands = orbitals.shape[0]
    slab = orbitals.shape[1]
    dom_count = lax.axis_size("dom")
    lower_cut = bounds[0]
    upper_cut = bounds[1]
    half_width = (upper_cut - lower_cut) / 2.0
    centre = (upper_cut + lower_cut) / 2.0
    slab_points = slab * GRID_Y * GRID_Z
    cell_volume = 1.0 / (slab_points * dom_count)
    start = orbitals.astype(jnp.float32)
    current, applied = slab_filter(start, potential, half_width, centre)
    filt_local = current.astype(jnp.bfloat16).reshape(local_bands, slab_points)
    applied_local = applied.astype(jnp.bfloat16).reshape(local_bands, slab_points)
    point_filt, point_applied = (
        lax.all_to_all(filt_local, "band", split_axis=1, concat_axis=0, tiled=True),
        lax.all_to_all(applied_local, "band", split_axis=1, concat_axis=0, tiled=True),
    )
    correlation, hamil_sub = gram_pair(point_filt, point_applied, cell_volume)
    scale = jnp.sqrt(jnp.sum(correlation * correlation) + 1e-06)
    high = lax.Precision.HIGHEST
    identity = jnp.eye(BANDS, dtype=jnp.float32)
    scaled = correlation / scale
    inverse = identity
    for repeat in range(NS_STEPS):
        factor = 1.5 * identity - 0.5 * jnp.dot(inverse, scaled, precision=high)
        scaled = jnp.dot(factor, scaled, precision=high)
        inverse = jnp.dot(factor, inverse, precision=high)
    transform = inverse / jnp.sqrt(scale)
    projected = jnp.dot(jnp.dot(transform.T, hamil_sub, precision=high), transform, precision=high)
    point_rotated = jnp.dot(transform.T, point_filt.astype(jnp.float32), precision=high).astype(
        jnp.bfloat16
    )
    band_rotated = lax.all_to_all(point_rotated, "band", split_axis=0, concat_axis=1, tiled=True)
    return (band_rotated.reshape(local_bands, slab, GRID_Y * GRID_Z), projected)


def solution(mesh):
    return jax.shard_map(
        body,
        mesh=mesh,
        in_specs=(P("band", "dom", None), P("dom", None), P()),
        out_specs=(P("band", "dom", None), P()),
        check_vma=False,
    )
```

profile of v0, /device:TPU:0, one launch (start us, length us, event | category | flops | bytes accessed | tf_op | source)
XLA Modules:
  0.0 625.8 jit_solution(11283899963984443685)
XLA Ops:
  22.4 5.1 collective-permute-done.1
  39.3 5.6 fusion.63
  53.6 11.0 %collective-permute-done.3 = f32[64,1,2048]{2,0,1:T(8,128)} collective-permute-done((f32[64,1,2048]{2,0,1:T(8,128)}, f32[64,1,2048]{2,0,1:T(8,128)}, u32[]{:S(2)}, u32[]{:S(2)}) %collective-permute-start.3) | collective-permute-done | bytes 524320 | tf_op jit(solution)/shard_map/ppermute | solution.py:22
  71.4 4.4 fusion.121
  77.3 7.8 %fusion.56 = f32[64,4,64,32]{0,3,2,1:T(8,128)} fusion(f32[64,6,64,32]{0,3,2,1:T(8,128)S(1)} %bitcast.143, f32[64,4,1,32]{0,3,2,1:T(8,128)S(1)} %get-tuple-element.67, f32[64,4,63,32]{0,3,2,1:T(8,128)} %get-tuple-element.69, f32[64,4,63,32]{0,3,2,1:T(8,128)} %get-tuple-element.68, f32[64,4,1,32]{0,3,2,1:T(8,128)S(1)} %get-tuple-element.66, ...), kind=kLoop, calls=%fused_computation.73 | loop fusion | flops 7340032 | bytes 16809984 | tf_op jit(solution)/shard_map/add | solution.py:42
  93.7 11.2 %collective-permute-done.5 = f32[64,1,2048]{2,0,1:T(8,128)S(1)} collective-permute-done((f32[64,1,2048]{2,0,1:T(8,128)S(1)}, f32[64,1,2048]{2,0,1:T(8,128)S(1)}, u32[]{:S(2)}, u32[]{:S(2)}) %collective-permute-start.5) | collective-permute-done | bytes 524320 | tf_op jit(solution)/shard_map/ppermute | solution.py:22
  108.4 4.4 fusion.117
  115.9 9.9 %fusion.49 = f32[64,4,64,32]{0,3,2,1:T(8,128)} fusion(f32[64,6,64,32]{0,3,2,1:T(8,128)S(1)} %bitcast.148, f32[64,4,1,32]{0,3,2,1:T(8,128)S(1)} %get-tuple-element.59, f32[64,4,63,32]{0,3,2,1:T(8,128)} %get-tuple-element.61, f32[64,4,63,32]{0,3,2,1:T(8,128)} %get-tuple-element.60, f32[64,4,1,32]{0,3,2,1:T(8,128)S(1)} %get-tuple-element.58, ...), kind=kLoop, calls=%fused_computation.65 | loop fusion | flops 7340032 | bytes 16809984 | tf_op jit(solution)/shard_map/add | solution.py:42
  133.5 11.4 %collective-permute-done.7 = f32[64,1,2048]{2,0,1:T(8,128)S(1)} collective-permute-done((f32[64,1,2048]{2,0,1:T(8,128)S(1)}, f32[64,1,2048]{2,0,1:T(8,128)S(1)}, u32[]{:S(2)}, u32[]{:S(2)}) %collective-permute-start.7) | collective-permute-done | bytes 524320 | tf_op jit(solution)/shard_map/ppermute | solution.py:22
  148.8 4.4 fusion.113
  156.2 9.9 %fusion.42 = f32[64,4,64,32]{0,3,2,1:T(8,128)} fusion(f32[64,6,64,32]{0,3,2,1:T(8,128)S(1)} %bitcast.153, f32[64,4,1,32]{0,3,2,1:T(8,128)S(1)} %get-tuple-element.51, f32[64,4,63,32]{0,3,2,1:T(8,128)} %get-tuple-element.53, f32[64,4,63,32]{0,3,2,1:T(8,128)} %get-tuple-element.52, f32[64,4,1,32]{0,3,2,1:T(8,128)S(1)} %get-tuple-element.50, ...), kind=kLoop, calls=%fused_computation.57 | loop fusion | flops 7340032 | bytes 16809984 | tf_op jit(solution)/shard_map/add | solution.py:42
  174.1 11.5 %collective-permute-done.9 = f32[64,1,2048]{2,0,1:T(8,128)S(1)} collective-permute-done((f32[64,1,2048]{2,0,1:T(8,128)S(1)}, f32[64,1,2048]{2,0,1:T(8,128)S(1)}, u32[]{:S(2)}, u32[]{:S(2)}) %collective-permute-start.9) | collective-permute-done | bytes 524320 | tf_op jit(solution)/shard_map/ppermute | solution.py:22
  189.1 4.4 fusion.109
  196.5 9.9 %fusion.35 = f32[64,4,64,32]{0,3,2,1:T(8,128)} fusion(f32[64,6,64,32]{0,3,2,1:T(8,128)S(1)} %bitcast.158, f32[64,4,1,32]{0,3,2,1:T(8,128)S(1)} %get-tuple-element.43, f32[64,4,63,32]{0,3,2,1:T(8,128)} %get-tuple-element.45, f32[64,4,63,32]{0,3,2,1:T(8,128)} %get-tuple-element.44, f32[64,4,1,32]{0,3,2,1:T(8,128)S(1)} %get-tuple-element.42, ...), kind=kLoop, calls=%fused_computation.49 | loop fusion | flops 7340032 | bytes 16809984 | tf_op jit(solution)/shard_map/add | solution.py:42
  214.5 11.7 %collective-permute-done.11 = f32[64,1,2048]{2,0,1:T(8,128)S(1)} collective-permute-done((f32[64,1,2048]{2,0,1:T(8,128)S(1)}, f32[64,1,2048]{2,0,1:T(8,128)S(1)}, u32[]{:S(2)}, u32[]{:S(2)}) %collective-permute-start.11) | collective-permute-done | bytes 524320 | tf_op jit(solution)/shard_map/ppermute | solution.py:22
  229.9 4.4 fusion.105
  237.4 9.9 %fusion.28 = f32[64,4,64,32]{0,3,2,1:T(8,128)} fusion(f32[64,6,64,32]{0,3,2,1:T(8,128)S(1)} %bitcast.163, f32[64,4,1,32]{0,3,2,1:T(8,128)S(1)} %get-tuple-element.35, f32[64,4,63,32]{0,3,2,1:T(8,128)} %get-tuple-element.37, f32[64,4,63,32]{0,3,2,1:T(8,128)} %get-tuple-element.36, f32[64,4,1,32]{0,3,2,1:T(8,128)S(1)} %get-tuple-element.34, ...), kind=kLoop, calls=%fused_computation.41 | loop fusion | flops 7340032 | bytes 16809984 | tf_op jit(solution)/shard_map/add | solution.py:42
  255.1 11.7 %collective-permute-done.13 = f32[64,1,2048]{2,0,1:T(8,128)S(1)} collective-permute-done((f32[64,1,2048]{2,0,1:T(8,128)S(1)}, f32[64,1,2048]{2,0,1:T(8,128)S(1)}, u32[]{:S(2)}, u32[]{:S(2)}) %collective-permute-start.13) | collective-permute-done | bytes 524320 | tf_op jit(solution)/shard_map/ppermute | solution.py:22
  270.4 4.4 fusion.101
  277.8 9.9 %fusion.21 = f32[64,4,64,32]{0,3,2,1:T(8,128)} fusion(f32[64,6,64,32]{0,3,2,1:T(8,128)S(1)} %bitcast.168, f32[64,4,1,32]{0,3,2,1:T(8,128)S(1)} %get-tuple-element.27, f32[64,4,63,32]{0,3,2,1:T(8,128)} %get-tuple-element.29, f32[64,4,63,32]{0,3,2,1:T(8,128)} %get-tuple-element.28, f32[64,4,1,32]{0,3,2,1:T(8,128)S(1)} %get-tuple-element.26, ...), kind=kLoop, calls=%fused_computation.33 | loop fusion | flops 7340032 | bytes 16809984 | tf_op jit(solution)/shard_map/add | solution.py:42
  295.7 11.7 %collective-permute-done.15 = f32[64,1,2048]{2,0,1:T(8,128)S(1)} collective-permute-done((f32[64,1,2048]{2,0,1:T(8,128)S(1)}, f32[64,1,2048]{2,0,1:T(8,128)S(1)}, u32[]{:S(2)}, u32[]{:S(2)}) %collective-permute-start.15) | collective-permute-done | bytes 524320 | tf_op jit(solution)/shard_map/ppermute | solution.py:22
  311.1 4.4 fusion.97
  318.6 9.9 %fusion.14 = f32[64,4,64,32]{0,3,2,1:T(8,128)} fusion(f32[64,6,64,32]{0,3,2,1:T(8,128)S(1)} %bitcast.173, f32[64,4,1,32]{0,3,2,1:T(8,128)S(1)} %get-tuple-element.19, f32[64,4,63,32]{0,3,2,1:T(8,128)} %get-tuple-element.21, f32[64,4,63,32]{0,3,2,1:T(8,128)} %get-tuple-element.20, f32[64,4,1,32]{0,3,2,1:T(8,128)S(1)} %get-tuple-element.18, ...), kind=kLoop, calls=%fused_computation.25 | loop fusion | flops 7340032 | bytes 16809984 | tf_op jit(solution)/shard_map/add | solution.py:42
  341.5 5.8 all-to-all-start
  347.3 3.6 collective-permute-done.17
  360.7 5.6 fusion.7
  367.9 5.4 all-to-all-done
  373.3 3.6 all-to-all-start.2
  379.1 23.8 %all-to-all-done.2 = bf16[64,8,1024]{2,0,1:T(8,128)(2,1)S(1)} async-done(((bf16[64,8,1024]{2,0,1:T(8,128)(2,1)}), bf16[64,8,1024]{2,0,1:T(8,128)(2,1)S(1)}, u32[]{:S(2)}, u32[]{:S(2)}) %all-to-all-start.2) | async-done | bytes 1048608 | tf_op jit(solution)/shard_map/all_to_all | solution.py:92
  404.6 134.3 %all-reduce.3.cloned.1.call-done = (f32[512,512]{1,0:T(8,128)}, f32[512,512]{1,0:T(8,128)}) async-done(((f32[512,512]{1,0:T(8,128)}, f32[512,512]{1,0:T(8,128)}), (f32[512,512]{1,0:T(8,128)}, f32[512,512]{1,0:T(8,128)})) %all-reduce.3.cloned.1.call-update) | async-done | bytes 2097168 | tf_op jit(solution)/shard_map/psum | solution.py:73
  587.7 4.3 all-to-all-start.1
  597.9 18.4 %all-to-all-done.1 = bf16[8,64,1024]{2,1,0:T(8,128)(2,1)S(1)} async-done(((bf16[8,64,1024]{2,1,0:T(8,128)(2,1)}), bf16[8,64,1024]{2,1,0:T(8,128)(2,1)S(1)}, u32[]{:S(2)}, u32[]{:S(2)}) %all-to-all-start.1) | async-done | bytes 1048608 | tf_op jit(solution)/shard_map/all_to_all | solution.py:109
  (205 shorter events, 213.9 us)
Async XLA Ops:
  13.5 14.0 %collective-permute-start.1 = (f32[64,1,2048]{2,0,1:T(8,128)}, f32[64,1,2048]{2,0,1:T(8,128)}, u32[]{:S(2)}, u32[]{:S(2)}) collective-permute-start(f32[64,1,2048]{2,0,1:T(8,128)} %copy.12), channel_id=1, source_target_pairs={{1,0},{2,1},{3,2},{0,3},{5,4},{6,5},{7,6},{4,7},{9,8},{10,9},{11,1... | collective-permute-start | bytes 1572872 | tf_op jit(solution)/shard_map/ppermute | solution.py:22
  17.1 12.5 %collective-permute-start = (f32[64,1,2048]{2,0,1:T(8,128)}, f32[64,1,2048]{2,0,1:T(8,128)}, u32[]{:S(2)}, u32[]{:S(2)}) collective-permute-start(f32[64,1,2048]{2,0,1:T(8,128)} %copy.11), channel_id=1, source_target_pairs={{0,1},{1,2},{2,3},{3,0},{4,5},{5,6},{6,7},{7,4},{8,9},{9,10},{10,1... | collective-permute-start | bytes 1572872 | tf_op jit(solution)/shard_map/ppermute | solution.py:20
  51.0 13.6 %collective-permute-start.3 = (f32[64,1,2048]{2,0,1:T(8,128)}, f32[64,1,2048]{2,0,1:T(8,128)}, u32[]{:S(2)}, u32[]{:S(2)}) collective-permute-start(f32[64,1,2048]{2,0,1:T(8,128)} %copy.16), channel_id=1, source_target_pairs={{1,0},{2,1},{3,2},{0,3},{5,4},{6,5},{7,6},{4,7},{9,8},{10,9},{11,1... | collective-permute-start | bytes 1572872 | tf_op jit(solution)/shard_map/ppermute | solution.py:22
  53.6 12.4 %collective-permute-start.2 = (f32[64,1,2048]{2,0,1:T(8,128)}, f32[64,1,2048]{2,0,1:T(8,128)}, u32[]{:S(2)}, u32[]{:S(2)}) collective-permute-start(f32[64,1,2048]{2,0,1:T(8,128)} %copy.15), channel_id=1, source_target_pairs={{0,1},{1,2},{2,3},{3,0},{4,5},{5,6},{6,7},{7,4},{8,9},{9,10},{10,1... | collective-permute-start | bytes 1572872 | tf_op jit(solution)/shard_map/ppermute | solution.py:20
  90.8 14.0 %collective-permute-start.5 = (f32[64,1,2048]{2,0,1:T(8,128)S(1)}, f32[64,1,2048]{2,0,1:T(8,128)S(1)}, u32[]{:S(2)}, u32[]{:S(2)}) collective-permute-start(f32[64,1,2048]{2,0,1:T(8,128)S(1)} %copy.20), channel_id=1, source_target_pairs={{1,0},{2,1},{3,2},{0,3},{5,4},{6,5},{7,6},{4,7},{9,8},{10,9},{11,1... | collective-permute-start | bytes 1572872 | tf_op jit(solution)/shard_map/ppermute | solution.py:22
  93.4 11.9 %collective-permute-start.4 = (f32[64,1,2048]{2,0,1:T(8,128)S(1)}, f32[64,1,2048]{2,0,1:T(8,128)S(1)}, u32[]{:S(2)}, u32[]{:S(2)}) collective-permute-start(f32[64,1,2048]{2,0,1:T(8,128)S(1)} %copy.19), channel_id=1, source_target_pairs={{0,1},{1,2},{2,3},{3,0},{4,5},{5,6},{6,7},{7,4},{8,9},{9,10},{10,1... | collective-permute-start | bytes 1572872 | tf_op jit(solution)/shard_map/ppermute | solution.py:20
  115.9 9.9 %copy-start.4 = (f32[64,4,2048]{0,2,1:T(8,128)S(1)}, f32[64,4,2048]{0,2,1:T(8,128)}, u32[]{:S(2)}) copy-start(f32[64,4,2048]{0,2,1:T(8,128)} %copy-done.3) | copy-start | bytes 6291460
  115.9 9.9 %copy-start.17 = (f32[64,4,2048]{0,2,1:T(8,128)S(1)}, f32[64,4,2048]{0,2,1:T(8,128)}, u32[]{:S(2)}) copy-start(f32[64,4,2048]{0,2,1:T(8,128)} %copy-done.15) | copy-start | bytes 6291460
  131.3 13.7 %collective-permute-start.7 = (f32[64,1,2048]{2,0,1:T(8,128)S(1)}, f32[64,1,2048]{2,0,1:T(8,128)S(1)}, u32[]{:S(2)}, u32[]{:S(2)}) collective-permute-start(f32[64,1,2048]{2,0,1:T(8,128)S(1)} %copy.24), channel_id=1, source_target_pairs={{1,0},{2,1},{3,2},{0,3},{5,4},{6,5},{7,6},{4,7},{9,8},{10,9},{11,1... | collective-permute-start | bytes 1572872 | tf_op jit(solution)/shard_map/ppermute | solution.py:22
  133.5 12.1 %collective-permute-start.6 = (f32[64,1,2048]{2,0,1:T(8,128)S(1)}, f32[64,1,2048]{2,0,1:T(8,128)S(1)}, u32[]{:S(2)}, u32[]{:S(2)}) collective-permute-start(f32[64,1,2048]{2,0,1:T(8,128)S(1)} %copy.23), channel_id=1, source_target_pairs={{0,1},{1,2},{2,3},{3,0},{4,5},{5,6},{6,7},{7,4},{8,9},{9,10},{10,1... | collective-permute-start | bytes 1572872 | tf_op jit(solution)/shard_map/ppermute | solution.py:20
  156.2 9.9 %copy-start.5 = (f32[64,4,2048]{0,2,1:T(8,128)S(1)}, f32[64,4,2048]{0,2,1:T(8,128)}, u32[]{:S(2)}) copy-start(f32[64,4,2048]{0,2,1:T(8,128)} %copy-done.3) | copy-start | bytes 6291460
  156.2 9.9 %copy-start.7 = (f32[64,4,2048]{0,2,1:T(8,128)S(1)}, f32[64,4,2048]{0,2,1:T(8,128)}, u32[]{:S(2)}) copy-start(f32[64,4,2048]{0,2,1:T(8,128)} %copy-done.6) | copy-start | bytes 6291460
  171.6 13.9 %collective-permute-start.9 = (f32[64,1,2048]{2,0,1:T(8,128)S(1)}, f32[64,1,2048]{2,0,1:T(8,128)S(1)}, u32[]{:S(2)}, u32[]{:S(2)}) collective-permute-start(f32[64,1,2048]{2,0,1:T(8,128)S(1)} %copy.28), channel_id=1, source_target_pairs={{1,0},{2,1},{3,2},{0,3},{5,4},{6,5},{7,6},{4,7},{9,8},{10,9},{11,1... | collective-permute-start | bytes 1572872 | tf_op jit(solution)/shard_map/ppermute | solution.py:22
  173.6 12.3 %collective-permute-start.8 = (f32[64,1,2048]{2,0,1:T(8,128)S(1)}, f32[64,1,2048]{2,0,1:T(8,128)S(1)}, u32[]{:S(2)}, u32[]{:S(2)}) collective-permute-start(f32[64,1,2048]{2,0,1:T(8,128)S(1)} %copy.27), channel_id=1, source_target_pairs={{0,1},{1,2},{2,3},{3,0},{4,5},{5,6},{6,7},{7,4},{8,9},{9,10},{10,1... | collective-permute-start | bytes 1572872 | tf_op jit(solution)/shard_map/ppermute | solution.py:20
  196.5 9.9 %copy-start.8 = (f32[64,4,2048]{0,2,1:T(8,128)S(1)}, f32[64,4,2048]{0,2,1:T(8,128)}, u32[]{:S(2)}) copy-start(f32[64,4,2048]{0,2,1:T(8,128)} %copy-done.6) | copy-start | bytes 6291460
  196.5 9.9 %copy-start.10 = (f32[64,4,2048]{0,2,1:T(8,128)S(1)}, f32[64,4,2048]{0,2,1:T(8,128)}, u32[]{:S(2)}) copy-start(f32[64,4,2048]{0,2,1:T(8,128)} %copy-done.9) | copy-start | bytes 6291460
  211.9 14.2 %collective-permute-start.11 = (f32[64,1,2048]{2,0,1:T(8,128)S(1)}, f32[64,1,2048]{2,0,1:T(8,128)S(1)}, u32[]{:S(2)}, u32[]{:S(2)}) collective-permute-start(f32[64,1,2048]{2,0,1:T(8,128)S(1)} %copy.32), channel_id=1, source_target_pairs={{1,0},{2,1},{3,2},{0,3},{5,4},{6,5},{7,6},{4,7},{9,8},{10,9},{11,1... | collective-permute-start | bytes 1572872 | tf_op jit(solution)/shard_map/ppermute | solution.py:22
  214.4 12.4 %collective-permute-start.10 = (f32[64,1,2048]{2,0,1:T(8,128)S(1)}, f32[64,1,2048]{2,0,1:T(8,128)S(1)}, u32[]{:S(2)}, u32[]{:S(2)}) collective-permute-start(f32[64,1,2048]{2,0,1:T(8,128)S(1)} %copy.31), channel_id=1, source_target_pairs={{0,1},{1,2},{2,3},{3,0},{4,5},{5,6},{6,7},{7,4},{8,9},{9,10},{10,1... | collective-permute-start | bytes 1572872 | tf_op jit(solution)/shard_map/ppermute | solution.py:20
  237.4 9.9 %copy-start.11 = (f32[64,4,2048]{0,2,1:T(8,128)S(1)}, f32[64,4,2048]{0,2,1:T(8,128)}, u32[]{:S(2)}) copy-start(f32[64,4,2048]{0,2,1:T(8,128)} %copy-done.9) | copy-start | bytes 6291460
  237.4 9.9 %copy-start.13 = (f32[64,4,2048]{0,2,1:T(8,128)S(1)}, f32[64,4,2048]{0,2,1:T(8,128)}, u32[]{:S(2)}) copy-start(f32[64,4,2048]{0,2,1:T(8,128)} %copy-done.12) | copy-start | bytes 6291460
  252.8 13.9 %collective-permute-start.13 = (f32[64,1,2048]{2,0,1:T(8,128)S(1)}, f32[64,1,2048]{2,0,1:T(8,128)S(1)}, u32[]{:S(2)}, u32[]{:S(2)}) collective-permute-start(f32[64,1,2048]{2,0,1:T(8,128)S(1)} %copy.36), channel_id=1, source_target_pairs={{1,0},{2,1},{3,2},{0,3},{5,4},{6,5},{7,6},{4,7},{9,8},{10,9},{11,1... | collective-permute-start | bytes 1572872 | tf_op jit(solution)/shard_map/ppermute | solution.py:22
  254.8 12.4 %collective-permute-start.12 = (f32[64,1,2048]{2,0,1:T(8,128)S(1)}, f32[64,1,2048]{2,0,1:T(8,128)S(1)}, u32[]{:S(2)}, u32[]{:S(2)}) collective-permute-start(f32[64,1,2048]{2,0,1:T(8,128)S(1)} %copy.35), channel_id=1, source_target_pairs={{0,1},{1,2},{2,3},{3,0},{4,5},{5,6},{6,7},{7,4},{8,9},{9,10},{10,1... | collective-permute-start | bytes 1572872 | tf_op jit(solution)/shard_map/ppermute | solution.py:20
  277.8 9.9 %copy-start.14 = (f32[64,4,2048]{0,2,1:T(8,128)S(1)}, f32[64,4,2048]{0,2,1:T(8,128)}, u32[]{:S(2)}) copy-start(f32[64,4,2048]{0,2,1:T(8,128)} %copy-done.12) | copy-start | bytes 6291460
  293.2 14.1 %collective-permute-start.15 = (f32[64,1,2048]{2,0,1:T(8,128)S(1)}, f32[64,1,2048]{2,0,1:T(8,128)S(1)}, u32[]{:S(2)}, u32[]{:S(2)}) collective-permute-start(f32[64,1,2048]{2,0,1:T(8,128)S(1)} %copy.40), channel_id=1, source_target_pairs={{1,0},{2,1},{3,2},{0,3},{5,4},{6,5},{7,6},{4,7},{9,8},{10,9},{11,1... | collective-permute-start | bytes 1572872 | tf_op jit(solution)/shard_map/ppermute | solution.py:22
  295.6 12.4 %collective-permute-start.14 = (f32[64,1,2048]{2,0,1:T(8,128)S(1)}, f32[64,1,2048]{2,0,1:T(8,128)S(1)}, u32[]{:S(2)}, u32[]{:S(2)}) collective-permute-start(f32[64,1,2048]{2,0,1:T(8,128)S(1)} %copy.39), channel_id=1, source_target_pairs={{0,1},{1,2},{2,3},{3,0},{4,5},{5,6},{6,7},{7,4},{8,9},{9,10},{10,1... | collective-permute-start | bytes 1572872 | tf_op jit(solution)/shard_map/ppermute | solution.py:20
  318.6 9.9 %copy-start.19 = (f32[64,4,2048]{0,2,1:T(8,128)S(1)}, f32[64,4,2048]{0,2,1:T(8,128)}, u32[]{:S(2)}) copy-start(f32[64,4,2048]{0,2,1:T(8,128)} %copy-done.18) | copy-start | bytes 6291460
  337.1 13.8 %collective-permute-start.17 = (f32[64,1,2048]{2,0,1:T(8,128)}, f32[64,1,2048]{2,0,1:T(8,128)}, u32[]{:S(2)}, u32[]{:S(2)}) collective-permute-start(f32[64,1,2048]{2,0,1:T(8,128)} %copy.46), channel_id=1, source_target_pairs={{1,0},{2,1},{3,2},{0,3},{5,4},{6,5},{7,6},{4,7},{9,8},{10,9},{11,1... | collective-permute-start | bytes 1572872 | tf_op jit(solution)/shard_map/ppermute | solution.py:22
  339.9 12.4 %collective-permute-start.16 = (f32[64,1,2048]{2,0,1:T(8,128)}, f32[64,1,2048]{2,0,1:T(8,128)}, u32[]{:S(2)}, u32[]{:S(2)}) collective-permute-start(f32[64,1,2048]{2,0,1:T(8,128)} %copy.45), channel_id=1, source_target_pairs={{0,1},{1,2},{2,3},{3,0},{4,5},{5,6},{6,7},{7,4},{8,9},{9,10},{10,1... | collective-permute-start | bytes 1572872 | tf_op jit(solution)/shard_map/ppermute | solution.py:20
  341.5 31.8 %all-to-all-start = ((bf16[64,8,1024]{2,0,1:T(8,128)(2,1)}), bf16[64,8,1024]{2,0,1:T(8,128)(2,1)S(1)}, u32[]{:S(2)}, u32[]{:S(2)}) async-start(bf16[64,8,1024]{2,0,1:T(8,128)(2,1)} %copy.43), calls=%async_computation | async-start | bytes 2097152 | tf_op jit(solution)/shard_map/all_to_all | solution.py:91
  373.3 29.6 %all-to-all-start.2 = ((bf16[64,8,1024]{2,0,1:T(8,128)(2,1)}), bf16[64,8,1024]{2,0,1:T(8,128)(2,1)S(1)}, u32[]{:S(2)}, u32[]{:S(2)}) async-start(bf16[64,8,1024]{2,0,1:T(8,128)(2,1)} %copy.49), calls=%async_computation.2 | async-start | bytes 2097152 | tf_op jit(solution)/shard_map/all_to_all | solution.py:92
  376.9 162.0 %all-reduce.3.cloned.1.call-start = ((), (), s32[]{:S(2)}) async-start(), calls=%async_computation.3 | async-start | bytes 4194304 | tf_op jit(solution)/shard_map/psum | solution.py:73
  587.7 28.6 %all-to-all-start.1 = ((bf16[8,64,1024]{2,1,0:T(8,128)(2,1)}), bf16[8,64,1024]{2,1,0:T(8,128)(2,1)S(1)}, u32[]{:S(2)}, u32[]{:S(2)}) async-start(bf16[8,64,1024]{2,1,0:T(8,128)(2,1)} %bitcast.21), calls=%async_computation.1 | async-start | bytes 2097152 | tf_op jit(solution)/shard_map/all_to_all | solution.py:109
  (14 other events, 64.8 us)
Sparse Core Ops, SparseCore 0:
  404.7 134.1 all-reduce.2
where the time goes:
time: 636 us; the launch traced here: 626 us
  waiting for transfers between devices  273 us (43%)
  other arithmetic  129 us (20%)
  local copies, waits for them, and re-layouts  118 us (19%)
  matrix products  54.9 us (9%)
  starting transfers between devices  32.6 us (5%)
  between operations  18.4 us (3%)
    psum x1, waiting for transfers between devices, gram_pair(): return lax.psum((correlation_part, hamil_part), ('band', 'dom'))  134 us
    ppermute x9, waiting for transfers between devices, padded(): lax.ppermute(head, axis, [((i + 1) % count, i) for i in range(count)])  88.7 us
    add x8, other arithmetic, stencil(): return -0.5 * (beside - 6.0 * middle) + pot_planes * middle  72.6 us
    slice x18, local copies, waits for them, and re-layouts, stencil(): beside = beside + jnp.roll(middle, -1, 2) + jnp.roll(middle, 1, 2)  36.5 us
    slice x18, local copies, waits for them, and re-layouts, stencil(): beside = beside + jnp.roll(middle, -1, 3) + jnp.roll(middle, 1, 3)  24.2 us
    concatenate x9, other arithmetic, padded(): jnp.concatenate([lax.ppermute(tail, axis, [(i, (i + 1) % count) for i in...  24 us
    all_to_all x1, waiting for transfers between devices, body(): lax.all_to_all(applied_local, 'band', split_axis=1, concat_axis=0, tiled=...  23.8 us
    unnamed x49, local copies, waits for them, and re-layouts  19.1 us
  transfers between devices with their start and end apart: 22, of which 19 were waited for; matrix products, arithmetic and copies ran while one was open for 6% of the time, Pallas kernels for 0%

commit v1 on v0

v1 whole, which is shorter than its diff:
```python
import functools

import jax
import jax.numpy as jnp
from jax import lax
from jax.experimental import pallas as pl
from jax.experimental.pallas import tpu as pltpu
from jax.sharding import PartitionSpec as P

GRID_Z = 32
DEG = 8
NS_STEPS = 8
LANES = 128


def filter_kernel(scal_ref, cells_ref, pot_ref, filt_ref, applied_ref, field, coef):
    planes, bands, width = cells_ref.shape
    blocks_per_plane = filt_ref.shape[0] // planes
    block = filt_ref.shape[2]
    rows = min(8, bands)
    chunks = width // LANES
    inv_half = scal_ref[0]
    centre = scal_ref[1]
    lane = lax.broadcasted_iota(jnp.int32, (rows, LANES), 1)
    z_cell = lane % GRID_Z
    z_last = z_cell == GRID_Z - 1
    z_first = z_cell == 0
    y_last = lane >= LANES - GRID_Z
    y_first = lane < GRID_Z

    def load(slot, x, start):
        return [
            field[slot, x, pl.ds(start, rows), pl.ds(c * LANES, LANES)] for c in range(chunks)
        ]

    def update(slot, x, start, weight, emit):
        before = lax.rem(x + planes - 1, planes)
        after = lax.rem(x + 1, planes)
        mine = load(slot, x, start)
        ups = [pltpu.roll(v, LANES - GRID_Z, 1) for v in mine]
        downs = [pltpu.roll(v, GRID_Z, 1) for v in mine]
        for c in range(chunks):
            v = mine[c]
            cols = pl.ds(c * LANES, LANES)
            total = field[slot, after, pl.ds(start, rows), cols]
            total = total + field[slot, before, pl.ds(start, rows), cols]
            total = total + jnp.where(y_last, ups[(c + 1) % chunks], ups[c])
            total = total + jnp.where(y_first, downs[(c - 1) % chunks], downs[c])
            total = total + jnp.where(
                z_last, pltpu.roll(v, GRID_Z - 1, 1), pltpu.roll(v, LANES - 1, 1)
            )
            total = total + jnp.where(
                z_first, pltpu.roll(v, LANES - GRID_Z + 1, 1), pltpu.roll(v, 1, 1)
            )
            emit(c, cols, v, weight * total)

    def sweep(step):
        def run(x, carry):
            for start in range(0, bands, rows):
                step(x, start)
            return carry

        lax.fori_loop(0, planes, run, 0)

    def setup(x, carry):
        field[0, x] = cells_ref[x].astype(jnp.float32)
        coef[x] = (3.0 + pot_ref[x] - centre) * (2.0 * inv_half)
        return carry

    lax.fori_loop(0, planes, setup, 0)

    def first(x, start):
        def emit(c, cols, v, part):
            field[1, x, pl.ds(start, rows), cols] = part + (0.5 * coef[x, :, cols]) * v

        update(0, x, start, -0.5 * inv_half, emit)

    sweep(first)

    def middle(k, carry):
        slot = lax.rem(k, 2)
        other = 1 - slot

        def step(x, start):
            def emit(c, cols, v, part):
                where = (other, x, pl.ds(start, rows), cols)
                field[where] = part + coef[x, :, cols] * v - field[where]

            update(slot, x, start, -inv_half, emit)

        sweep(step)
        return carry

    lax.fori_loop(1, DEG, middle, 0)
    last_slot = DEG % 2

    def last(x, carry):
        for start in range(0, bands, rows):

            def emit(c, cols, v, part):
                piece = (c * LANES) // block
                inner = (c * LANES) % block
                where = (
                    x * blocks_per_plane + piece,
                    pl.ds(start, rows),
                    pl.ds(inner, LANES),
                )
                filt_ref[where] = v.astype(jnp.bfloat16)
                applied_ref[where] = (part + (3.0 + pot_ref[x, :, cols]) * v).astype(jnp.bfloat16)

            update(last_slot, x, start, -0.5, emit)
        return carry

    lax.fori_loop(0, planes, last, 0)


def filter_bands(cells, potential, scalars, devices):
    planes, bands, width = cells.shape
    block = planes * width // devices
    out = jax.ShapeDtypeStruct((devices, bands, block), jnp.bfloat16)
    vmem = pl.BlockSpec(memory_space=pltpu.VMEM)
    return pl.pallas_call(
        filter_kernel,
        out_shape=(out, out),
        in_specs=[pl.BlockSpec(memory_space=pltpu.SMEM), vmem, vmem],
        out_specs=(vmem, vmem),
        scratch_shapes=[
            pltpu.VMEM((2, planes, bands, width), jnp.float32),
            pltpu.VMEM((planes, 1, width), jnp.float32),
        ],
        compiler_params=pltpu.CompilerParams(vmem_limit_bytes=32 << 20),
    )(scalars, cells, potential)


def split(value):
    high = value.astype(jnp.bfloat16)
    return high, (value - high.astype(jnp.float32)).astype(jnp.bfloat16)


def dot(a, b):
    return jnp.dot(a, b, preferred_element_type=jnp.float32)


def dot3(a, b):
    (a_high, a_low), (b_high, b_low) = a, b
    return dot(a_high, b_high) + (dot(a_high, b_low) + dot(a_low, b_high))


def rotate_kernel(groups, corr_ref, hamil_ref, filt_ref, out_ref, proj_ref, y_ref, z_ref, t_ref):
    size = corr_ref.shape[0]
    outer, inner, width = groups
    row = lax.broadcasted_iota(jnp.int32, (size, size), 0)
    col = lax.broadcasted_iota(jnp.int32, (size, size), 1)
    diag = jnp.where(row == col, 1.5, 0.0)
    corr = corr_ref[...]
    scale = jnp.sqrt(jnp.sum(corr * corr) + 1e-06)
    scaled = corr / scale
    factor = diag - 0.5 * scaled
    z_ref[...] = factor
    y_ref[...] = dot3(split(factor), split(scaled))

    def step(k, carry):
        y = split(y_ref[...])
        z = split(z_ref[...])
        factor = split(diag - 0.5 * dot3(z, y))
        y_ref[...] = dot3(factor, y)
        z_ref[...] = dot3(factor, z)
        return carry

    lax.fori_loop(1, NS_STEPS - 1, step, 0)
    y = split(y_ref[...])
    z = split(z_ref[...])
    factor = split(diag - 0.5 * dot3(z, y))
    t_ref[...] = dot3(factor, z) / jnp.sqrt(scale)
    for i in range(outer):
        for j in range(inner):
            z_ref[pl.ds((j * outer + i) * width, width), :] = t_ref[
                pl.ds((i * inner + j) * width, width), :
            ]
    trans = split(z_ref[...])
    half = split(dot3(trans, split(hamil_ref[...])))
    contract = (((1,), (1,)), ((), ()))

    def dot_t(a, b):
        return lax.dot_general(a, b, contract, preferred_element_type=jnp.float32)

    proj_ref[...] = dot_t(half[0], trans[0]) + (
        dot_t(half[0], trans[1]) + dot_t(half[1], trans[0])
    )
    filt = filt_ref[...]
    out_ref[...] = (dot(trans[0], filt) + dot(trans[1], filt)).astype(jnp.bfloat16)


def rotate(corr, hamil, filt, groups):
    size = corr.shape[0]
    vmem = pl.BlockSpec(memory_space=pltpu.VMEM)
    square = pltpu.VMEM((size, size), jnp.float32)
    return pl.pallas_call(
        functools.partial(rotate_kernel, groups),
        out_shape=(
            jax.ShapeDtypeStruct(filt.shape, jnp.bfloat16),
            jax.ShapeDtypeStruct(corr.shape, jnp.float32),
        ),
        in_specs=[vmem] * 3,
        out_specs=(vmem, vmem),
        scratch_shapes=[square] * 3,
        compiler_params=pltpu.CompilerParams(vmem_limit_bytes=40 << 20),
    )(corr, hamil, filt)


def body(orbitals, potential, bounds):
    bands, slab, width = orbitals.shape
    doms = lax.axis_size("dom")
    groups = lax.axis_size("band")
    devices = doms * groups
    total_bands = bands * groups
    mine = bands // doms
    everyone = ("dom", "band")
    half_width = (bounds[1] - bounds[0]) / 2.0
    centre = (bounds[1] + bounds[0]) / 2.0
    cell_volume = 1.0 / (slab * doms * width)

    sent = orbitals.reshape(doms, mine, slab, width).transpose(0, 2, 1, 3)
    cells = lax.all_to_all(sent, "dom", split_axis=0, concat_axis=0, tiled=True)
    cells = cells.reshape(doms * slab, mine, width)
    pot = lax.all_to_all(
        jnp.broadcast_to(potential, (doms, slab, width)), "dom", split_axis=0, concat_axis=0, tiled=True
    ).reshape(doms * slab, 1, width)
    filt, applied = filter_bands(cells, pot, jnp.stack([1.0 / half_width, centre]), devices)
    filt = lax.all_to_all(filt, everyone, split_axis=0, concat_axis=0, tiled=True)
    applied = lax.all_to_all(applied, everyone, split_axis=0, concat_axis=0, tiled=True)
    filt = filt.reshape(total_bands, -1)
    applied = applied.reshape(total_bands, -1)
    contract = (((1,), (1,)), ((), ()))

    def summed(other):
        part = lax.dot_general(filt, other, contract, preferred_element_type=jnp.float32)
        part = part.astype(jnp.bfloat16).reshape(devices, total_bands // devices, total_bands)
        part = lax.all_to_all(part, everyone, split_axis=0, concat_axis=0, tiled=True)
        return jnp.sum(part.astype(jnp.float32), axis=0) * cell_volume

    corr = lax.all_gather(summed(filt), everyone, axis=0, tiled=True)
    hamil = lax.all_gather(summed(applied), everyone, axis=0, tiled=True)
    rotated, projected = rotate(corr, hamil, filt, (doms, groups, mine))
    out = lax.all_to_all(rotated, "band", split_axis=0, concat_axis=1, tiled=True)
    return out.reshape(bands, slab, width), projected


def solution(mesh):
    return jax.shard_map(
        body,
        mesh=mesh,
        in_specs=(P("band", "dom", None), P("dom", None), P()),
        out_specs=(P("band", "dom", None), P()),
        check_vma=False,
    )
```

time: 636 us -> 357 us (0.56); the launches traced: 626 us -> 356 us
  waiting for transfers between devices: 273 us -> 101 us
  blocking collectives: 0 us -> 130 us
  other arithmetic: 129 us -> 1.48 us
  local copies, waits for them, and re-layouts: 118 us -> 9.62 us
  Pallas kernels: 0 us -> 88 us
  matrix products: 54.9 us -> 1.48 us
  starting transfers between devices: 32.6 us -> 8 us
    psum x1 -> x0, waiting for transfers between devices: 134 us -> none  [gram_pair(): return lax.psum((correlation_part, hamil_part), ('band', 'dom'))]
    all_to_all x0 -> x5, blocking collectives: none -> 130 us  [the longest x2 37.5 us: summed(): lax.all_to_all(part, everyone, split_axis=0, concat_axis=0, tiled=True)]
    ppermute x18 -> x0, waiting for transfers between devices: 90.7 us -> none  [the longest x9 88.7 us: padded(): lax.ppermute(head, axis, [((i + 1) % count, i) for i in range(count)])]
    pallas_call x0 -> x2, Pallas kernels: none -> 88 us  [the longest x1 66.3 us: filter_bands(): pl.pallas_call(filter_kernel, out_shape=(out, out), in_specs=[pl.BlockSpe...]
    all_gather x0 -> x2, waiting for transfers between devices: none -> 87.9 us  [the longest x1 56.4 us: body(): corr = lax.all_gather(summed(filt), everyone, axis=0, tiled=True)]
    slice x64 -> x1, local copies, waits for them, and re-layouts: 79.5 us -> 0.61 us  [body(): half_width = (bounds[1] - bounds[0]) / 2.0]
    add x8 -> x0, other arithmetic: 72.6 us -> none  [stencil(): return -0.5 * (beside - 6.0 * middle) + pot_planes * middle]
    dot_general x28 -> x2, matrix products: 54.9 us -> 1.48 us  [summed(): lax.dot_general(filt, other, contract, preferred_element_type=jnp.float32)]
  transfers between devices with their start and end apart: 22 -> 4, of which waited for: 19 -> 4; matrix products, arithmetic and copies ran while one was open for 6% -> 1% of each run, Pallas kernels for 0% -> 0%
where the time goes in v1:
time: 357 us; the launch traced here: 356 us
  blocking collectives  130 us (36%)
  waiting for transfers between devices  101 us (28%)
  Pallas kernels  88 us (25%)
  between operations  16.7 us (5%)
  local copies, waits for them, and re-layouts  9.62 us (3%)
  starting transfers between devices  8 us (2%)
    pallas_call x1, Pallas kernels, filter_bands(): pl.pallas_call(filter_kernel, out_shape=(out, out), in_specs=[pl.BlockSpe...  66.3 us
    all_gather x1, waiting for transfers between devices, body(): corr = lax.all_gather(summed(filt), everyone, axis=0, tiled=True)  56.4 us
    all_to_all x2, blocking collectives, summed(): lax.all_to_all(part, everyone, split_axis=0, concat_axis=0, tiled=True)  37.5 us
    all_to_all x1, blocking collectives, body(): lax.all_to_all(filt, everyone, split_axis=0, concat_axis=0, tiled=True)  32.7 us
    all_gather x1, waiting for transfers between devices, body(): hamil = lax.all_gather(summed(applied), everyone, axis=0, tiled=True)  31.5 us
    all_to_all x1, blocking collectives, body(): lax.all_to_all(rotated, 'band', split_axis=0, concat_axis=1, tiled=True)  30.2 us
    all_to_all x1, blocking collectives, body(): lax.all_to_all(applied, everyone, split_axis=0, concat_axis=0, tiled=True)  29.7 us
    pallas_call x1, Pallas kernels, rotate(): pl.pallas_call(functools.partial(rotate_kernel, groups), out_shape=(jax.S...  21.7 us
  transfers between devices with their start and end apart: 4, of which 4 were waited for; matrix products, arithmetic and copies ran while one was open for 1% of the time, Pallas kernels for 0%

profile of v1, /device:TPU:0, one launch (start us, length us, event | category | flops | bytes accessed | tf_op | source)
XLA Modules:
  0.0 356.0 jit_solution(5144650277492920226)
XLA Ops:
  7.2 1.4 broadcast_in_dim.3
  8.6 4.3 %all-to-all-start.1 = ((f32[4,4,2048]{2,1,0:T(4,128)}), f32[4,4,2048]{2,1,0:T(4,128)S(1)}, u32[]{:S(2)}, u32[]{:S(2)}) async-start(f32[4,4,2048]{2,1,0:T(4,128)} %broadcast_in_dim.3), calls=%async_computation.1 | async-start | bytes 262144 | tf_op jit(solution)/shard_map/all_to_all | solution.py:226
  12.9 2.8 copy.8
  15.6 1.8 all-to-all-done.1
  17.5 3.6 %all-to-all-start = ((bf16[4,4,16,2048]{3,2,1,0:T(8,128)(2,1)}), bf16[4,4,16,2048]{3,2,1,0:T(8,128)(2,1)S(1)}, u32[]{:S(2)}, u32[]{:S(2)}) async-start(bf16[4,4,16,2048]{3,2,1,0:T(8,128)(2,1)} %bitcast.14), calls=%async_computation | async-start | bytes 2097152 | tf_op jit(solution)/shard_map/all_to_all | solution.py:224
  21.1 0.0 all-gather.5.cloned.1.call-start
  21.2 0.6 fusion
  24.4 0.1 pad_maximum_fusion.scal_ref
  24.5 0.2 reshape.44.pot_ref
  24.6 10.9 %all-to-all-done = bf16[4,4,16,2048]{3,2,1,0:T(8,128)(2,1)S(1)} async-done(((bf16[4,4,16,2048]{3,2,1,0:T(8,128)(2,1)}), bf16[4,4,16,2048]{3,2,1,0:T(8,128)(2,1)S(1)}, u32[]{:S(2)}, u32[]{:S(2)}) %all-to-all-start) | async-done | bytes 1048608 | tf_op jit(solution)/shard_map/all_to_all | solution.py:224
  35.5 66.3 %shard_map.50 = (bf16[32,16,1024]{2,1,0:T(8,128)(2,1)S(1)}, bf16[32,16,1024]{2,1,0:T(8,128)(2,1)S(1)}) custom-call(f32[2]{0:T(128)S(1)} %pad_maximum_fusion.scal_ref, bf16[16,16,2048]{2,1,0:T(8,128)(2,1)S(1)} %bitcast.18, f32[16,1,2048]{2,1,0:T(1,128)S(1)} %reshape.44.pot_ref), custom_call_target="tpu_custom_call" | custom-call | tf_op jit(solution)/shard_map/pallas_call | solution.py:122
  101.8 32.7 %all_to_all.46 = bf16[32,16,1024]{2,1,0:T(8,128)(2,1)S(1)} all-to-all(bf16[32,16,1024]{2,1,0:T(8,128)(2,1)S(1)} %get-tuple-element.6), channel_id=1, replica_groups=mesh['band'=8,'dom'=4] {'dom','band'}, dimensions={0} | all-to-all | bytes 2097152 | tf_op jit(solution)/shard_map/all_to_all | solution.py:230
  134.5 29.7 %all_to_all.47 = bf16[32,16,1024]{2,1,0:T(8,128)(2,1)S(1)} all-to-all(bf16[32,16,1024]{2,1,0:T(8,128)(2,1)S(1)} %get-tuple-element.7), channel_id=1, replica_groups=mesh['band'=8,'dom'=4] {'dom','band'}, dimensions={0} | all-to-all | bytes 2097152 | tf_op jit(solution)/shard_map/all_to_all | solution.py:231
  164.2 0.7 convolution_convert_fusion
  164.9 18.5 %all_to_all.48 = bf16[32,16,512]{2,1,0:T(8,128)(2,1)S(1)} all-to-all(bf16[32,16,512]{2,1,0:T(8,128)(2,1)S(1)} %bitcast.23), channel_id=1, replica_groups=mesh['band'=8,'dom'=4] {'dom','band'}, dimensions={0} | all-to-all | bytes 1048576 | tf_op jit(solution)/shard_map/all_to_all | solution.py:239
  183.4 0.1 convert_reduce_fusion
  183.5 0.6 broadcast_multiply_fusion
  184.1 0.0 all-gather.5.cloned.1.call-update
  184.2 0.0 all-gather.3.cloned.1.call-start
  184.2 0.7 convolution_convert_fusion.1
  185.0 19.0 %all_to_all.49 = bf16[32,16,512]{2,1,0:T(8,128)(2,1)S(1)} all-to-all(bf16[32,16,512]{2,1,0:T(8,128)(2,1)S(1)} %bitcast.24), channel_id=1, replica_groups=mesh['band'=8,'dom'=4] {'dom','band'}, dimensions={0} | all-to-all | bytes 1048576 | tf_op jit(solution)/shard_map/all_to_all | solution.py:239
  204.0 0.1 convert_reduce_fusion.1
  204.0 0.6 broadcast_multiply_fusion.1
  204.7 0.0 all-gather.3.cloned.1.call-update
  204.7 31.5 %all-gather.5.cloned.1.call-done.hamil_ref = f32[512,512]{1,0:T(8,128)} async-done(((f32[16,512]{1,0:T(8,128)}), f32[512,512]{1,0:T(8,128)}) %all-gather.5.cloned.1.call-update) | async-done | bytes 1048592 | tf_op jit(solution)/shard_map/all_gather | solution.py:243
  236.2 56.4 %all-gather.3.cloned.1.call-done.corr_ref = f32[512,512]{1,0:T(8,128)} async-done(((f32[16,512]{1,0:T(8,128)}), f32[512,512]{1,0:T(8,128)}) %all-gather.3.cloned.1.call-update) | async-done | bytes 1048592 | tf_op jit(solution)/shard_map/all_gather | solution.py:242
  292.6 1.2 copy-done
  293.8 1.2 copy-done.1
  295.0 21.7 %shard_map.51 = (bf16[512,1024]{1,0:T(8,128)(2,1)S(1)}, f32[512,512]{1,0:T(8,128)}) custom-call(f32[512,512]{1,0:T(8,128)S(1)} %copy-done.1, f32[512,512]{1,0:T(8,128)S(1)} %copy-done, bf16[512,1024]{1,0:T(8,128)(2,1)S(1)} %bitcast.17), custom_call_target="tpu_custom_call" | custom-call | tf_op jit(solution)/shard_map/pallas_call | solution.py:198
  316.8 30.2 %all_to_all.50 = bf16[8,64,1024]{2,1,0:T(8,128)(2,1)S(1)} all-to-all(bf16[8,64,1024]{2,1,0:T(8,128)(2,1)S(1)} %bitcast.19), channel_id=1, replica_groups=mesh['band'=8,'dom'=4] {'band'}, dimensions={0} | all-to-all | bytes 2097152 | tf_op jit(solution)/shard_map/all_to_all | solution.py:245
  347.0 0.6 copy.6
  347.6 1.6 reshape.49
  (4 shorter events, 0.0 us)
Async XLA Ops:
  8.6 8.9 %all-to-all-start.1 = ((f32[4,4,2048]{2,1,0:T(4,128)}), f32[4,4,2048]{2,1,0:T(4,128)S(1)}, u32[]{:S(2)}, u32[]{:S(2)}) async-start(f32[4,4,2048]{2,1,0:T(4,128)} %broadcast_in_dim.3), calls=%async_computation.1 | async-start | bytes 262144 | tf_op jit(solution)/shard_map/all_to_all | solution.py:226
  17.5 3.7 %copy-start.2 = (f32[2]{0:T(128)S(1)}, f32[2]{0:T(128)}, u32[]{:S(2)}) copy-start(f32[2]{0:T(128)} %param.5) | copy-start | bytes 28
  17.5 18.1 %all-to-all-start = ((bf16[4,4,16,2048]{3,2,1,0:T(8,128)(2,1)}), bf16[4,4,16,2048]{3,2,1,0:T(8,128)(2,1)S(1)}, u32[]{:S(2)}, u32[]{:S(2)}) async-start(bf16[4,4,16,2048]{3,2,1,0:T(8,128)(2,1)} %bitcast.14), calls=%async_computation | async-start | bytes 2097152 | tf_op jit(solution)/shard_map/all_to_all | solution.py:224
  21.1 215.1 %all-gather.5.cloned.1.call-start = ((), (), s32[]{:S(2)}) async-start(), calls=%async_computation.8 | async-start | bytes 1081344 | tf_op jit(solution)/shard_map/all_gather | solution.py:243
  184.2 108.4 %all-gather.3.cloned.1.call-start = ((), (), s32[]{:S(2)}) async-start(), calls=%async_computation.7 | async-start | bytes 1081344 | tf_op jit(solution)/shard_map/all_gather | solution.py:242
  292.6 1.2 copy-start
  293.8 1.2 copy-start.1
Sparse Core Ops, SparseCore 0:
  184.3 51.8 all-gather.4
  239.8 52.7 all-gather.2

commit v2 on v1

v2 whole, which is shorter than its diff:
```python
import functools

import jax
import jax.numpy as jnp
from jax import lax
from jax.experimental import pallas as pl
from jax.experimental.pallas import tpu as pltpu
from jax.sharding import PartitionSpec as P

GRID_Z = 32
DEG = 8
NS_STEPS = 8
LANES = 128
TILE_ROWS = 16


def filter_kernel(scal_ref, cells_ref, pot_ref, sums_ref, filt_ref, applied_ref, field, high, low, coef):
    planes, bands, width = cells_ref.shape
    rows = planes * bands
    blocks_per_plane = filt_ref.shape[0] // planes
    block = filt_ref.shape[2]
    tile = sums_ref.shape[1]
    inv_half = scal_ref[0]
    centre = scal_ref[1]

    for x in range(planes):
        mine = pl.ds(x * bands, bands)
        coef[mine, :] = jnp.broadcast_to(3.0 + pot_ref[x], (bands, width))
        start = cells_ref[x].astype(jnp.float32)
        field[0, mine, :] = start
    for c in range(width // tile):
        cols = pl.ds(c * tile, tile)
        start = field[0, :, cols]
        high[0, :, cols] = start.astype(jnp.bfloat16)
        low[0, :, cols] = jnp.zeros((rows, tile), jnp.bfloat16)

    def shifted(v, by):
        if bands % 8 == 0:
            return jnp.concatenate([v[by:], v[:by]], axis=0)
        return pltpu.roll(v, (rows - by) % rows, 0)

    def neighbours(slot, c, v):
        cols = pl.ds(pl.multiple_of(c * tile, tile), tile)
        left = pl.ds(pl.multiple_of(lax.rem(c * tile + width - LANES, width), LANES), LANES)
        right = pl.ds(pl.multiple_of(lax.rem(c * tile + tile, width), LANES), LANES)

        def part(ref):
            wide = jnp.concatenate([ref[slot, :, left], ref[slot, :, cols], ref[slot, :, right]], axis=1)
            return dot(wide, sums_ref[...])

        return part(high) + part(low) + (shifted(v, bands) + shifted(v, rows - bands))

    def sweep(slot, other, weight, diagonal, first):
        def run(c, carry):
            cols = pl.ds(pl.multiple_of(c * tile, tile), tile)
            v = field[slot, :, cols]
            fresh = weight * neighbours(slot, c, v) + (coef[:, cols] * diagonal[0] + diagonal[1]) * v
            if not first:
                fresh = fresh - field[other, :, cols]
            field[other, :, cols] = fresh
            top, rest = split(fresh)
            high[other, :, cols] = top
            low[other, :, cols] = rest
            return carry

        lax.fori_loop(0, width // tile, run, 0)

    sweep(0, 1, -0.5 * inv_half, (inv_half, -centre * inv_half), True)

    def middle(k, carry):
        slot = lax.rem(k, 2)
        sweep(slot, 1 - slot, -inv_half, (2.0 * inv_half, -2.0 * centre * inv_half), False)
        return carry

    lax.fori_loop(1, DEG, middle, 0)
    slot = DEG % 2
    for c in range(width // tile):
        cols = pl.ds(c * tile, tile)
        v = field[slot, :, cols]
        applied = coef[:, cols] * v - 0.5 * neighbours(slot, c, v)
        piece, inner = divmod(c * tile, block)
        for x in range(planes):
            where = (x * blocks_per_plane + piece, slice(None), pl.ds(inner, tile))
            filt_ref[where] = v[x * bands : (x + 1) * bands].astype(jnp.bfloat16)
            applied_ref[where] = applied[x * bands : (x + 1) * bands].astype(jnp.bfloat16)


def neighbour_sums(tile):
    source = lax.broadcasted_iota(jnp.int32, (tile + 2 * LANES, tile), 0) - LANES
    target = lax.broadcasted_iota(jnp.int32, (tile + 2 * LANES, tile), 1)
    step = source - target
    same_row = (source >= 0) & (source // GRID_Z == target // GRID_Z)
    apart = lax.rem(step + GRID_Z, GRID_Z)
    beside_z = same_row & ((apart == 1) | (apart == GRID_Z - 1))
    beside_y = (step == GRID_Z) | (step == -GRID_Z)
    return (beside_z | beside_y).astype(jnp.bfloat16)


def filter_bands(cells, potential, scalars, devices):
    planes, bands, width = cells.shape
    rows = planes * bands
    block = planes * width // devices
    out = jax.ShapeDtypeStruct((devices, bands, block), jnp.bfloat16)
    vmem = pl.BlockSpec(memory_space=pltpu.VMEM)
    return pl.pallas_call(
        filter_kernel,
        out_shape=(out, out),
        in_specs=[pl.BlockSpec(memory_space=pltpu.SMEM), vmem, vmem, vmem],
        out_specs=(vmem, vmem),
        scratch_shapes=[
            pltpu.VMEM((2, rows, width), jnp.float32),
            pltpu.VMEM((2, rows, width), jnp.bfloat16),
            pltpu.VMEM((2, rows, width), jnp.bfloat16),
            pltpu.VMEM((rows, width), jnp.float32),
        ],
        compiler_params=pltpu.CompilerParams(vmem_limit_bytes=48 << 20),
    )(scalars, cells, potential, neighbour_sums(min(256, block)))


def split(value):
    spread = value * 65537.0
    high = spread - (spread - value)
    return high.astype(jnp.bfloat16), (value - high).astype(jnp.bfloat16)


def dot(a, b):
    return jnp.dot(a, b, preferred_element_type=jnp.float32)


def dot3(a, b):
    (a_high, a_low), (b_high, b_low) = a, b
    return dot(a_high, b_high) + (dot(a_high, b_low) + dot(a_low, b_high))


def exchange_bits(doms, groups):
    dom = [("dom", 1 << i) for i in range(1, (doms - 1).bit_length())]
    band = [("band", 1 << i) for i in range((groups - 1).bit_length())]
    core = [("dom", 1)]
    return core + band[:1] + dom + band[1:], core + dom + band


def reduce_kernel(
    bits, cell_volume, groups,
    filt_ref, applied_ref, out_ref, proj_ref,
    total, send, recv, gath, y_ref, z_ref, t_ref, send_sem, recv_sem,
):
    size = filt_ref.shape[0]
    index = {axis: lax.axis_index(axis) for axis in ("dom", "band")}

    def partner(axis, bit):
        mine = lax.rem(index[axis] // bit, 2)
        return mine, {axis: index[axis] + bit - 2 * bit * mine}

    barrier = pltpu.get_barrier_semaphore()
    for axis, bit in bits[0]:
        pl.semaphore_signal(
            barrier, inc=1, device_id=partner(axis, bit)[1], device_id_type=pl.DeviceIdType.MESH
        )

    pairs = (((1,), (1,)), ((), ()))
    for stream, other in enumerate((filt_ref, applied_ref)):
        for lead in range(0, size, 256):
            total[stream, pl.ds(lead, 256), :] = cell_volume * lax.dot_general(
                filt_ref[pl.ds(lead, 256), :], other[...], pairs, preferred_element_type=jnp.float32
            )
    pl.semaphore_wait(barrier, len(bits[0]))

    def copy(stream, number, source, target, device):
        made = pltpu.make_async_remote_copy(
            src_ref=source,
            dst_ref=target,
            send_sem=send_sem.at[stream, number],
            recv_sem=recv_sem.at[stream, number],
            device_id=device,
            device_id_type=pl.DeviceIdType.MESH,
        )
        made.start()
        return made

    stages = len(bits[0])
    start = [jnp.int32(0)] * 2
    halved = [[], []]
    length, offset = size, 0
    for stage in range(stages):
        halve = length >= 2 * TILE_ROWS
        count = length // 2 if halve else length
        space = pl.ds(offset, count)
        flight = []
        for stream in range(2):
            axis, bit = bits[stream][stage]
            mine, device = partner(axis, bit)
            give = start[stream] + (1 - mine) * count if halve else start[stream]
            keep = start[stream] + mine * count if halve else start[stream]
            give = pl.multiple_of(give, TILE_ROWS)
            send[stream, space, :] = total[stream, pl.ds(give, count), :]
            flight.append(
                copy(stream, stage, send.at[stream, space], recv.at[stream, space], device)
            )
            start[stream] = pl.multiple_of(keep, TILE_ROWS)
            if halve:
                halved[stream].append((stage, mine, device))
        for stream in range(2):
            flight[stream].wait()
            kept = pl.ds(start[stream], count)
            if halve:
                own = total[stream, kept, :]
            else:
                own = send[stream, space, :]
            total[stream, kept, :] = own + recv[stream, space, :]
        length = count
        offset += count

    for stream in range(2):
        kept = pl.ds(start[stream], length)
        gath[stream, kept, :] = total[stream, kept, :]
    for back in range(len(halved[0]) - 1, -1, -1):
        flight = []
        for stream in range(2):
            stage, mine, device = halved[stream][back]
            area = gath.at[stream, pl.ds(start[stream], length)]
            flight.append(copy(stream, stages + stage, area, area, device))
            start[stream] = pl.multiple_of(start[stream] - mine * length, TILE_ROWS)
        for made in flight:
            made.wait()
        length *= 2

    outer, inner, width = groups
    row = lax.broadcasted_iota(jnp.int32, (size, size), 0)
    col = lax.broadcasted_iota(jnp.int32, (size, size), 1)
    diag = jnp.where(row == col, 1.5, 0.0)
    corr = gath[0]
    scale = jnp.sqrt(jnp.sum(corr * corr) + 1e-06)
    scaled = corr / scale
    factor = diag - 0.5 * scaled
    z_ref[...] = factor
    y_ref[...] = dot3(split(factor), split(scaled))

    def step(k, carry):
        y = split(y_ref[...])
        z = split(z_ref[...])
        factor = split(diag - 0.5 * dot3(z, y))
        y_ref[...] = dot3(factor, y)
        z_ref[...] = dot3(factor, z)
        return carry

    lax.fori_loop(1, NS_STEPS - 1, step, 0)
    y = split(y_ref[...])
    z = split(z_ref[...])
    factor = split(diag - 0.5 * dot3(z, y))
    t_ref[...] = dot3(factor, z) / jnp.sqrt(scale)
    for i in range(outer):
        for j in range(inner):
            z_ref[pl.ds((j * outer + i) * width, width), :] = t_ref[
                pl.ds((i * inner + j) * width, width), :
            ]
    trans = split(z_ref[...])
    half = split(dot3(trans, split(gath[1])))
    contract = (((1,), (1,)), ((), ()))

    def dot_t(a, b):
        return lax.dot_general(a, b, contract, preferred_element_type=jnp.float32)

    proj_ref[...] = dot_t(half[0], trans[0]) + (
        dot_t(half[0], trans[1]) + dot_t(half[1], trans[0])
    )
    filt = filt_ref[...]
    out_ref[...] = (dot(trans[0], filt) + dot(trans[1], filt)).astype(jnp.bfloat16)


def rotate(filt, applied, cell_volume, groups):
    size = filt.shape[0]
    bits = exchange_bits(groups[0], groups[1])
    vmem = pl.BlockSpec(memory_space=pltpu.VMEM)
    square = pltpu.VMEM((size, size), jnp.float32)
    room = size + TILE_ROWS * len(bits[0])
    sems = pltpu.SemaphoreType.DMA((2, 2 * len(bits[0])))
    return pl.pallas_call(
        functools.partial(reduce_kernel, bits, cell_volume, groups),
        out_shape=(
            jax.ShapeDtypeStruct(filt.shape, jnp.bfloat16),
            jax.ShapeDtypeStruct((size, size), jnp.float32),
        ),
        in_specs=[vmem] * 2,
        out_specs=(vmem, vmem),
        scratch_shapes=[
            pltpu.VMEM((2, size, size), jnp.float32),
            pltpu.VMEM((2, room, size), jnp.float32),
            pltpu.VMEM((2, room, size), jnp.float32),
            pltpu.VMEM((2, size, size), jnp.float32),
            square,
            square,
            square,
            sems,
            sems,
        ],
        compiler_params=pltpu.CompilerParams(
            vmem_limit_bytes=56 << 20, collective_id=0, has_side_effects=True
        ),
    )(filt, applied)


def body(orbitals, potential, bounds):
    bands, slab, width = orbitals.shape
    doms = lax.axis_size("dom")
    groups = lax.axis_size("band")
    devices = doms * groups
    total_bands = bands * groups
    mine = bands // doms
    everyone = ("dom", "band")
    half_width = (bounds[1] - bounds[0]) / 2.0
    centre = (bounds[1] + bounds[0]) / 2.0
    cell_volume = 1.0 / (slab * doms * width)

    sent = orbitals.reshape(doms, mine, slab, width).transpose(0, 2, 1, 3)
    cells = lax.all_to_all(sent, "dom", split_axis=0, concat_axis=0, tiled=True)
    cells = cells.reshape(doms * slab, mine, width)
    pot = lax.all_to_all(
        jnp.broadcast_to(potential, (doms, slab, width)), "dom", split_axis=0, concat_axis=0, tiled=True
    ).reshape(doms * slab, 1, width)
    filt, applied = filter_bands(cells, pot, jnp.stack([1.0 / half_width, centre]), devices)
    filt = lax.all_to_all(filt, everyone, split_axis=0, concat_axis=0, tiled=True)
    applied = lax.all_to_all(applied, everyone, split_axis=0, concat_axis=0, tiled=True)
    filt = filt.reshape(total_bands, -1)
    applied = applied.reshape(total_bands, -1)
    rotated, projected = rotate(filt, applied, cell_volume, (doms, groups, mine))
    out = lax.all_to_all(rotated, "band", split_axis=0, concat_axis=1, tiled=True)
    return out.reshape(bands, slab, width), projected


def solution(mesh):
    return jax.shard_map(
        body,
        mesh=mesh,
        in_specs=(P("band", "dom", None), P("dom", None), P()),
        out_specs=(P("band", "dom", None), P()),
        check_vma=False,
    )
```

time: 357 us -> 223 us (0.62)
  blocking collectives: 130 us -> 62.7 us
  waiting for transfers between devices: 101 us -> 39.8 us
  between operations: 16.7 us -> 3.19 us
  Pallas kernels: 88 us -> 96 us
    all_gather x2 -> x0, waiting for transfers between devices: 87.9 us -> none  [the longest x1 56.4 us: body(): corr = lax.all_gather(summed(filt), everyone, axis=0, tiled=True)]
    all_to_all x3 -> x0, blocking collectives: 67.7 us -> none  [the longest x2 37.5 us: summed(): lax.all_to_all(part, everyone, split_axis=0, concat_axis=0, tiled=True)]
    pallas_call x1, Pallas kernels: 21.7 us -> 70.9 us  [rotate(): pl.pallas_call(functools.partial(reduce_kernel, bits, cell_volume, groups...]
    pallas_call x1, Pallas kernels: 66.3 us -> 25 us  [filter_bands(): pl.pallas_call(filter_kernel, out_shape=(out, out), in_specs=[pl.BlockSpe...]
    all_to_all x0 -> x1, waiting for transfers between devices: none -> 26.4 us  [body(): lax.all_to_all(rotated, 'band', split_axis=0, concat_axis=1, tiled=True)]
  transfers between devices with their start and end apart: 4 -> 3, of which waited for: 4 -> 2; matrix products, arithmetic and copies ran while one was open for 1% -> 2% of each run, Pallas kernels for 0% -> 0%
where the time goes in v2:
time: 223 us; the launch traced here: 222 us
  Pallas kernels  96 us (43%)
  blocking collectives  62.7 us (28%)
  waiting for transfers between devices  39.8 us (18%)
  starting transfers between devices  11.5 us (5%)
  local copies, waits for them, and re-layouts  8.13 us (4%)
  between operations  3.19 us (1%)
    pallas_call x1, Pallas kernels, rotate(): pl.pallas_call(functools.partial(reduce_kernel, bits, cell_volume, groups...  70.9 us
    all_to_all x1, blocking collectives, body(): lax.all_to_all(filt, everyone, split_axis=0, concat_axis=0, tiled=True)  32.8 us
    all_to_all x1, blocking collectives, body(): lax.all_to_all(applied, everyone, split_axis=0, concat_axis=0, tiled=True)  29.9 us
    all_to_all x1, waiting for transfers between devices, body(): lax.all_to_all(rotated, 'band', split_axis=0, concat_axis=1, tiled=True)  26.4 us
    pallas_call x1, Pallas kernels, filter_bands(): pl.pallas_call(filter_kernel, out_shape=(out, out), in_specs=[pl.BlockSpe...  25 us
    all_to_all x1, waiting for transfers between devices, body(): cells = lax.all_to_all(sent, 'dom', split_axis=0, concat_axis=0, tiled=True)  13.4 us
  transfers between devices with their start and end apart: 3, of which 2 were waited for; matrix products, arithmetic and copies ran while one was open for 2% of the time, Pallas kernels for 0%

profile of v2, /device:TPU:0, one launch (start us, length us, event | category | flops | bytes accessed | tf_op | source)
XLA Modules:
  0.0 222.1 jit_solution(5443414849565610400)
XLA Ops:
  0.6 1.4 broadcast_in_dim.3
  2.1 0.0 copy-start.1
  2.1 4.4 %all-to-all-start.1 = ((f32[4,4,2048]{2,1,0:T(4,128)}), f32[4,4,2048]{2,1,0:T(4,128)S(1)}, u32[]{:S(2)}, u32[]{:S(2)}) async-start(f32[4,4,2048]{2,1,0:T(4,128)} %broadcast_in_dim.3), calls=%async_computation.1 | async-start | bytes 262144 | tf_op jit(solution)/shard_map/all_to_all | solution.py:317
  6.5 0.0 copy-done.1
  6.5 0.6 fusion.12
  9.5 2.8 %copy.8 = bf16[4,16,4,2048]{3,1,2,0:T(8,128)(2,1)} copy(bf16[4,16,4,2048]{3,2,1,0:T(4,128)(2,1)} %bitcast.13) | data formatting | bytes 2097152 | tf_op jit(solution)/shard_map/reshape | solution.py:314
  12.3 0.0 all-to-all-done.1
  12.3 3.5 %all-to-all-start = ((bf16[4,4,16,2048]{3,2,1,0:T(8,128)(2,1)}), bf16[4,4,16,2048]{3,2,1,0:T(8,128)(2,1)S(1)}, u32[]{:S(2)}, u32[]{:S(2)}) async-start(bf16[4,4,16,2048]{3,2,1,0:T(8,128)(2,1)} %bitcast.8), calls=%async_computation | async-start | bytes 2097152 | tf_op jit(solution)/shard_map/all_to_all | solution.py:315
  15.9 0.1 pad_maximum_fusion.scal_ref
  16.0 0.7 fusion.6.sums_ref
  16.7 0.2 reshape.38.pot_ref
  16.9 13.4 %all-to-all-done = bf16[4,4,16,2048]{3,2,1,0:T(8,128)(2,1)S(1)} async-done(((bf16[4,4,16,2048]{3,2,1,0:T(8,128)(2,1)}), bf16[4,4,16,2048]{3,2,1,0:T(8,128)(2,1)S(1)}, u32[]{:S(2)}, u32[]{:S(2)}) %all-to-all-start) | async-done | bytes 1048608 | tf_op jit(solution)/shard_map/all_to_all | solution.py:315
  30.3 25.0 %shard_map.50 = (bf16[32,16,1024]{2,1,0:T(8,128)(2,1)S(1)}, bf16[32,16,1024]{2,1,0:T(8,128)(2,1)S(1)}) custom-call(f32[2]{0:T(128)S(1)} %pad_maximum_fusion.scal_ref, bf16[16,16,2048]{2,1,0:T(8,128)(2,1)S(1)} %bitcast.9, f32[16,1,2048]{2,1,0:T(1,128)S(1)} %reshape.38.pot_ref, bf16[512,256]{1,0:T(8,128)(2,1)S(1)} %fusion.6.sums_ref), custom_call_target="tpu_custom_call" | custom-call | tf_op jit(solution)/shard_map/pallas_call | solution.py:105
  55.3 32.8 %all_to_all.36 = bf16[32,16,1024]{2,1,0:T(8,128)(2,1)} all-to-all(bf16[32,16,1024]{2,1,0:T(8,128)(2,1)S(1)} %get-tuple-element.6), channel_id=1, replica_groups=mesh['band'=8,'dom'=4] {'dom','band'}, dimensions={0} | all-to-all | bytes 2097152 | tf_op jit(solution)/shard_map/all_to_all | solution.py:321
  88.1 29.9 %all_to_all.37 = bf16[32,16,1024]{2,1,0:T(8,128)(2,1)} all-to-all(bf16[32,16,1024]{2,1,0:T(8,128)(2,1)S(1)} %get-tuple-element.7), channel_id=1, replica_groups=mesh['band'=8,'dom'=4] {'dom','band'}, dimensions={0} | all-to-all | bytes 2097152 | tf_op jit(solution)/shard_map/all_to_all | solution.py:322
  118.0 70.9 %shard_map.51 = (bf16[512,1024]{1,0:T(8,128)(2,1)}, f32[512,512]{1,0:T(8,128)}) custom-call(bf16[512,1024]{1,0:T(8,128)(2,1)} %bitcast.11, bf16[512,1024]{1,0:T(8,128)(2,1)} %bitcast.12), custom_call_target="tpu_custom_call" | custom-call | tf_op jit(solution)/shard_map/pallas_call | solution.py:277
  188.9 3.6 %all-to-all-start.4 = ((bf16[8,64,1024]{2,1,0:T(8,128)(2,1)}), bf16[8,64,1024]{2,1,0:T(8,128)(2,1)S(1)}, u32[]{:S(2)}, u32[]{:S(2)}) async-start(bf16[8,64,1024]{2,1,0:T(8,128)(2,1)} %bitcast.14), calls=%async_computation.4 | async-start | bytes 2097152 | tf_op jit(solution)/shard_map/all_to_all | solution.py:326
  192.5 26.4 %all-to-all-done.4 = bf16[8,64,1024]{2,1,0:T(8,128)(2,1)S(1)} async-done(((bf16[8,64,1024]{2,1,0:T(8,128)(2,1)}), bf16[8,64,1024]{2,1,0:T(8,128)(2,1)S(1)}, u32[]{:S(2)}, u32[]{:S(2)}) %all-to-all-start.4) | async-done | bytes 1048608 | tf_op jit(solution)/shard_map/all_to_all | solution.py:326
  218.9 0.6 copy.6
  219.5 0.0 copy-start
  219.5 1.6 reshape.41
  221.1 0.0 copy-done
  221.1 1.0 copy.10
  (5 shorter events, 0.0 us)
Async XLA Ops:
  2.1 4.4 %copy-start.1 = (f32[2]{0:T(128)S(1)}, f32[2]{0:T(128)}, u32[]{:S(2)}) copy-start(f32[2]{0:T(128)} %param.5) | copy-start | bytes 28
  2.1 10.2 %all-to-all-start.1 = ((f32[4,4,2048]{2,1,0:T(4,128)}), f32[4,4,2048]{2,1,0:T(4,128)S(1)}, u32[]{:S(2)}, u32[]{:S(2)}) async-start(f32[4,4,2048]{2,1,0:T(4,128)} %broadcast_in_dim.3), calls=%async_computation.1 | async-start | bytes 262144 | tf_op jit(solution)/shard_map/all_to_all | solution.py:317
  12.3 17.9 %all-to-all-start = ((bf16[4,4,16,2048]{3,2,1,0:T(8,128)(2,1)}), bf16[4,4,16,2048]{3,2,1,0:T(8,128)(2,1)S(1)}, u32[]{:S(2)}, u32[]{:S(2)}) async-start(bf16[4,4,16,2048]{3,2,1,0:T(8,128)(2,1)} %bitcast.8), calls=%async_computation | async-start | bytes 2097152 | tf_op jit(solution)/shard_map/all_to_all | solution.py:315
  188.9 30.0 %all-to-all-start.4 = ((bf16[8,64,1024]{2,1,0:T(8,128)(2,1)}), bf16[8,64,1024]{2,1,0:T(8,128)(2,1)S(1)}, u32[]{:S(2)}, u32[]{:S(2)}) async-start(bf16[8,64,1024]{2,1,0:T(8,128)(2,1)} %bitcast.14), calls=%async_computation.4 | async-start | bytes 2097152 | tf_op jit(solution)/shard_map/all_to_all | solution.py:326
  219.5 1.6 copy-start
